TPU v7x, 512 devices: a whole 4x4x16 slice. The times are simulated.
512 devices in a mesh: dp: 64 (over x, z_lo, core), mp: 8 (over y, z_hi).
Axes of the slice: x: 4, y: 4, z: 16 (z_hi: 2, z_lo: 8; z = z_hi * 8 + z_lo), core: 2. Of those that a mesh axis runs over, the one named last changes fastest.
Arguments:
- states: bfloat16 [128, 64, 2048], P('dp', None, 'mp'), may hold values from -6 to 6
- w_qkv: bfloat16 [3, 2048, 2048], P(None, 'dp', 'mp'), may hold values from -0.125 to 0.125
- w_out: bfloat16 [2048, 2048], P('dp', 'mp'), may hold values from -0.125 to 0.125
- cache_keys: bfloat16 [128, 384, 2048], P('dp', None, 'mp'), as said below
- cache_values: bfloat16 [128, 384, 2048], P('dp', None, 'mp'), may hold values from -6 to 6
- parents: int32 [128, 64], P('dp'), may hold values from 0 to 62, as said below
- accept: int32 [128, 8], P('dp'), may hold values from 0 to 63, as said below
- lengths: int32 [128], replicated, may hold values from 48 to 384
- perm: int32 [128], replicated, may hold values from 0 to 127, each once
Outputs:
- tree_out: bfloat16 [128, 64, 2048], P('dp', None, 'mp')
- new_keys: bfloat16 [128, 8, 2048], P('dp', None, 'mp')
- new_values: bfloat16 [128, 8, 2048], P('dp', None, 'mp')
Inputs may be any that keep to these rules, and one draw needn't show every extreme that they name: parents[r, 0] = 0 for the root and parents[r, i] < i for every other node. `accept`: each row is a chain of 8 nodes from the root (node 0) downward, each entry the parent of the next. `perm`: each request stands in exactly one slot. `cache_keys`: keys of earlier positions, already rotated; slots at or past the request's length hold arbitrary values.
All inputs are finite; a program needn't handle non-finite values.
Results may differ from a plain program's by a relative error of at most 0.012.
The roundings to bfloat16 on the way count: a program that leaves them out, or rounds other values in their place, can miss the bound.
Values may be sent and summed in bfloat16 or wider, within the bound.
A program may use at most 64 MiB of HBM per device.

v0:
```python
import jax
import jax.numpy as jnp
from jax import lax
from jax.sharding import PartitionSpec as P

HEAD_DIM = 128


EPSILON = 1e-05
ROPE_BASE = 10000.0
NEG_FILL = -1e30


def layer_norm(rows):
    mean_val = jnp.mean(rows, axis=-1, keepdims=True)
    centred = rows - mean_val
    variance = jnp.mean(centred * centred, axis=-1, keepdims=True)
    return centred * lax.rsqrt(variance + EPSILON)


def rotate(values, position):
    half = values.shape[-1] // 2
    freqs = ROPE_BASE ** (-(jnp.arange(half, dtype=jnp.float32) * 2.0 / values.shape[-1]))
    angle = position[:, :, None, None] * freqs
    cosine = jnp.cos(angle)
    sine = jnp.sin(angle)
    first = values[..., :half]
    second = values[..., half:]
    return jnp.concatenate(
        [first * cosine - second * sine, second * cosine + first * sine], axis=-1
    )


def closure(parents):
    tree_len = parents.shape[-1]
    node_ids = jnp.arange(tree_len, dtype=jnp.int32)
    linked = (parents[:, :, None] == node_ids[None, None, :]) & (node_ids[None, :, None] > 0)
    reach = jnp.eye(tree_len, dtype=jnp.float32)[None] + linked.astype(jnp.float32)
    covered = 1
    while covered < tree_len:
        reach = jnp.minimum(jnp.einsum("rij,rjk->rik", reach, reach), 1.0)
        covered = covered * 2
    return reach


def local(states, w_qkv, w_out, cache_keys, cache_values, parents, accept, lengths, perm):
    req_count, tree_len, local_dim = states.shape
    cache_len = cache_keys.shape[1]
    heads_here = local_dim // HEAD_DIM
    scale = HEAD_DIM ** (-0.5)
    flat_rows = req_count * tree_len
    gathered = lax.all_gather(states, "mp", axis=2, tiled=True)
    normed = layer_norm(gathered.astype(jnp.float32)).astype(jnp.bfloat16).reshape(flat_rows, -1)

    def add_one(piece):
        return jnp.dot(normed, piece, preferred_element_type=jnp.float32)

    query_flat = add_one(lax.all_gather(w_qkv[0], "dp", axis=0, tiled=True))
    key_flat = add_one(lax.all_gather(w_qkv[1], "dp", axis=0, tiled=True))
    value_flat = add_one(lax.all_gather(w_qkv[2], "dp", axis=0, tiled=True))
    dealt_ids = lax.dynamic_slice_in_dim(perm, lax.axis_index("dp") * req_count, req_count)
    matches = dealt_ids[:, None] == jnp.arange(perm.shape[0], dtype=jnp.int32)[None, :]
    own_lengths = jnp.sum(jnp.where(matches, lengths[None, :], 0), axis=1)
    reach = closure(parents)
    depth = jnp.sum(reach, axis=-1) - 1.0
    position = own_lengths.astype(jnp.float32)[:, None] + depth
    shape_heads = (req_count, tree_len, heads_here, HEAD_DIM)
    queries = rotate(query_flat.reshape(shape_heads), position).astype(jnp.bfloat16)
    keys_new = rotate(key_flat.reshape(shape_heads), position).astype(jnp.bfloat16)
    values_new = value_flat.reshape(shape_heads).astype(jnp.bfloat16)
    keys_old = cache_keys.reshape(req_count, cache_len, heads_here, HEAD_DIM)
    values_old = cache_values.reshape(req_count, cache_len, heads_here, HEAD_DIM)
    tree_scores = (
        jnp.einsum("rthd,rshd->rhts", queries, keys_new, preferred_element_type=jnp.float32) * scale
    )
    tree_scores = jnp.where(reach[:, None] > 0, tree_scores, NEG_FILL)
    cache_scores = (
        jnp.einsum("rthd,rchd->rhtc", queries, keys_old, preferred_element_type=jnp.float32) * scale
    )
    valid = jnp.arange(cache_len, dtype=jnp.int32)[None, :] < own_lengths[:, None]
    cache_scores = jnp.where(valid[:, None, None, :], cache_scores, NEG_FILL)
    peak = jnp.maximum(jnp.max(cache_scores, axis=-1), jnp.max(tree_scores, axis=-1))
    cache_exp = jnp.exp(cache_scores - peak[..., None])
    tree_exp = jnp.exp(tree_scores - peak[..., None])
    denom = jnp.sum(cache_exp, axis=-1) + jnp.sum(tree_exp, axis=-1)
    cache_prob = (cache_exp / denom[..., None]).astype(jnp.bfloat16)
    tree_prob = (tree_exp / denom[..., None]).astype(jnp.bfloat16)
    mixed = jnp.einsum(
        "rhtc,rchd->rthd", cache_prob, values_old, preferred_element_type=jnp.float32
    )
    mixed = mixed + jnp.einsum(
        "rhts,rshd->rthd", tree_prob, values_new, preferred_element_type=jnp.float32
    )
    attended = mixed.astype(jnp.bfloat16).reshape(flat_rows, local_dim)
    heads_all = lax.all_gather(attended, "mp", axis=1, tiled=True)
    projected_out = jnp.dot(
        heads_all,
        lax.all_gather(w_out, "dp", axis=0, tiled=True),
        preferred_element_type=jnp.float32,
    )
    tree_out = (
        states.astype(jnp.float32) + projected_out.reshape(req_count, tree_len, local_dim)
    ).astype(jnp.bfloat16)
    picker = (accept[:, :, None] == jnp.arange(tree_len, dtype=jnp.int32)[None, None, :]).astype(
        jnp.bfloat16
    )
    stacked = jnp.concatenate(
        [
            keys_new.reshape(req_count, tree_len, local_dim),
            values_new.reshape(req_count, tree_len, local_dim),
        ],
        axis=-1,
    )
    chosen = jnp.einsum("rdt,rtn->rdn", picker, stacked, preferred_element_type=jnp.float32).astype(
        jnp.bfloat16
    )
    return (tree_out, chosen[..., :local_dim], chosen[..., local_dim:])


def solution(mesh):
    in_specs = (
        P("dp", None, "mp"),
        P(None, "dp", "mp"),
        P("dp", "mp"),
        P("dp", None, "mp"),
        P("dp", None, "mp"),
        P("dp", None),
        P("dp", None),
        P(),
        P(),
    )
    out_specs = (P("dp", None, "mp"), P("dp", None, "mp"), P("dp", None, "mp"))
    return jax.shard_map(local, mesh=mesh, in_specs=in_specs, out_specs=out_specs, check_vma=False)
```

profile of v0, /device:TPU:6, one launch (start us, length us, event | category | flops | bytes accessed | tf_op | source)
XLA Modules:
  0.0 532.3 jit_solution(12800749686257656289)
XLA Ops:
  7.2 1.4 fusion.52
  8.7 0.7 all-gather.10.cloned.1.call-update
  9.5 0.7 all-gather.12.cloned.1.call-update
  10.2 0.5 all-gather.8.cloned.1.call-update
  10.8 0.6 copy-done.6
  11.5 0.6 copy-done.7
  12.3 91.3 %all_gather.18 = bf16[2,64,2048]{2,1,0:T(8,128)(2,1)S(1)} all-gather(bf16[2,64,256]{2,1,0:T(8,128)(2,1)S(1)} %copy-done.2), channel_id=1, replica_groups=mesh['dp'=64,'mp'=8] {'mp'}, dimensions={2}, use_global_device_ids=true | all-gather | bytes 589824 | tf_op jit(solution)/shard_map/all_gather | solution.py:52
  103.8 0.3 fusion.6
  104.1 0.7 copy-done.4
  104.8 0.4 convolution_minimum_fusion.4
  105.2 0.3 convolution_minimum_fusion.2
  105.5 0.4 fusion.54
  106.1 0.3 multiply_cosine_fusion
  106.4 42.2 %all-gather.14.cloned.1.call-done = bf16[1,2048,256]{2,1,0:T(8,128)(2,1)} async-done(((bf16[1,32,256]{2,1,0:T(8,128)(2,1)}), bf16[1,2048,256]{2,1,0:T(8,128)(2,1)}) %all-gather.14.cloned.1.call-update) | async-done | bytes 1048592 | tf_op jit(solution)/shard_map/all_gather | solution.py:60
  148.6 1.5 copy.36
  150.1 119.4 %all-gather.10.cloned.1.call-done = bf16[1,2048,256]{2,1,0:T(8,128)(2,1)} async-done(((bf16[1,32,256]{2,1,0:T(8,128)(2,1)}), bf16[1,2048,256]{2,1,0:T(8,128)(2,1)}) %all-gather.10.cloned.1.call-update) | async-done | bytes 1048592 | tf_op jit(solution)/shard_map/all_gather | solution.py:58
  269.5 1.5 copy.29
  271.0 116.4 %all-gather.12.cloned.1.call-done = bf16[1,2048,256]{2,1,0:T(8,128)(2,1)} async-done(((bf16[1,32,256]{2,1,0:T(8,128)(2,1)}), bf16[1,2048,256]{2,1,0:T(8,128)(2,1)}) %all-gather.12.cloned.1.call-update) | async-done | bytes 1048592 | tf_op jit(solution)/shard_map/all_gather | solution.py:59
  387.4 2.3 copy.34
  389.7 0.5 fusion.42
  390.2 0.7 copy-done.1
  390.9 0.5 fusion.40
  391.9 0.4 fusion.55
  392.7 0.5 convolution_convert_fusion
  393.4 0.8 copy-done.3
  394.2 0.3 fusion.5
  394.6 79.3 %all_gather.22 = bf16[128,2048]{1,0:T(8,128)(2,1)S(1)} all-gather(bf16[128,256]{1,0:T(8,128)(2,1)S(1)} %bitcast.82), channel_id=1, replica_groups=mesh['dp'=64,'mp'=8] {'mp'}, dimensions={1}, use_global_device_ids=true | all-gather | bytes 589824 | tf_op jit(solution)/shard_map/all_gather | solution.py:95
  473.9 48.2 %all-gather.8.cloned.1.call-done = bf16[2048,256]{1,0:T(8,128)(2,1)} async-done(((bf16[32,256]{1,0:T(8,128)(2,1)}), bf16[2048,256]{1,0:T(8,128)(2,1)}) %all-gather.8.cloned.1.call-update) | async-done | bytes 1048592 | tf_op jit(solution)/shard_map/all_gather | solution.py:98
  522.1 1.5 fusion.58
  523.6 0.6 add_convert_fusion
  524.3 0.7 copy-done.5
  525.1 0.6 fusion.53
  (40 shorter events, 2.2 us)
Async XLA Ops:
  7.2 384.8 %copy-start = (bf16[2,384,256]{2,1,0:T(8,128)(2,1)S(1)}, bf16[2,384,256]{2,1,0:T(8,128)(2,1)}, u32[]{:S(2)}) copy-start(bf16[2,384,256]{2,1,0:T(8,128)(2,1)} %param.12) | copy-start | bytes 1179652
  7.2 141.4 %all-gather.14.cloned.1.call-start = ((), (), s32[]{:S(2)}) async-start(), calls=%async_computation.3 | async-start | bytes 1064960 | tf_op jit(solution)/shard_map/all_gather | solution.py:60
  8.6 3.7 copy-start.2
  8.7 260.8 %all-gather.10.cloned.1.call-start = ((), (), s32[]{:S(2)}) async-start(), calls=%async_computation.1 | async-start | bytes 1064960 | tf_op jit(solution)/shard_map/all_gather | solution.py:58
  9.4 378.0 %all-gather.12.cloned.1.call-start = ((), (), s32[]{:S(2)}) async-start(), calls=%async_computation.2 | async-start | bytes 1064960 | tf_op jit(solution)/shard_map/all_gather | solution.py:59
  10.1 511.9 %all-gather.8.cloned.1.call-start = ((), (), s32[]{:S(2)}) async-start(), calls=%async_computation | async-start | bytes 1064960 | tf_op jit(solution)/shard_map/all_gather | solution.py:98
  10.8 0.7 copy-start.6
  11.4 0.7 copy-start.7
  104.1 0.7 copy-start.4
  389.7 1.2 copy-start.1
  393.2 1.0 copy-start.3
  524.3 0.7 copy-start.5
Sparse Core Ops, SparseCore 0:
  10.1 138.4 all-gather.13
  151.3 118.1 all-gather.9
  271.7 115.7 all-gather.11
  389.5 132.5 all-gather.7
where the time goes:
time: 534 us; the launch traced here: 532 us
  waiting for transfers between devices  328 us (61%)
  blocking collectives  171 us (32%)
  between operations  14 us (3%)
  local copies, waits for them, and re-layouts  11.6 us (2%)
  matrix products  5.43 us (1%)
    all_gather x1, waiting for transfers between devices, local(): query_flat = add_one(lax.all_gather(w_qkv[0], 'dp', axis=0, tiled=True))  119 us
    all_gather x1, waiting for transfers between devices, local(): key_flat = add_one(lax.all_gather(w_qkv[1], 'dp', axis=0, tiled=True))  116 us
    all_gather x1, blocking collectives, local(): gathered = lax.all_gather(states, 'mp', axis=2, tiled=True)  91.3 us
    all_gather x1, blocking collectives, local(): heads_all = lax.all_gather(attended, 'mp', axis=1, tiled=True)  79.3 us
    all_gather x1, waiting for transfers between devices, local(): lax.all_gather(w_out, 'dp', axis=0, tiled=True)  48.2 us
    all_gather x1, waiting for transfers between devices, local(): value_flat = add_one(lax.all_gather(w_qkv[2], 'dp', axis=0, tiled=True))  42.2 us
  transfers between devices with their start and end apart: 4, of which 4 were waited for; matrix products, arithmetic and copies ran while one was open for 2% of the time, Pallas kernels for 0%

commit v1 on v0

v1 whole, which is shorter than its diff:
```python
import functools

import jax
import jax.numpy as jnp
import numpy as np
from jax import lax
from jax.experimental import pallas as pl
from jax.experimental.pallas import tpu as pltpu
from jax.sharding import PartitionSpec as P

HEAD_DIM = 128
EPSILON = 1e-05
ROPE_BASE = 10000.0
NEG_FILL = -1e30
MESH = pl.DeviceIdType.MESH
F32 = jnp.float32
BF16 = jnp.bfloat16


def mod4(value):
    return lax.rem(value + 8, 4)


class Links:
    def __init__(self):
        self.started = []

    def send(self, view, send_sem, recv_sem, device):
        copy = pltpu.make_async_remote_copy(
            src_ref=view, dst_ref=view, send_sem=send_sem, recv_sem=recv_sem,
            device_id=device, device_id_type=MESH,
        )
        copy.start()
        self.started.append(copy)

    def arrive(self, view, send_sem, recv_sem, device):
        pltpu.make_async_remote_copy(
            src_ref=view, dst_ref=view, send_sem=send_sem, recv_sem=recv_sem,
            device_id=device, device_id_type=MESH,
        ).wait_recv()

    def drain(self):
        for copy in self.started:
            copy.wait_send()


class Gather:
    def __init__(self, links, place, shard, batch, zs, zr, xs, xr, cs, cr):
        self.links, self.place, self.shard, self.batch = links, place, shard, batch
        self.zs, self.zr, self.xs, self.xr, self.cs, self.cr = zs, zr, xs, xr, cs, cr

    def z_source(self, index):
        p = self.place
        group = p.g if index < 4 else 1 - p.g
        return group * 4 + mod4(p.q - index % 4)

    def x_source(self, step):
        return mod4(self.place.x - step)

    def view(self, index, step, core):
        return self.shard(self.x_source(step) * 8 + self.z_source(index), core)

    def to_group(self, base):
        p = self.place
        for k in (1, 2, 3):
            device = p.at(zl=p.g * 4 + mod4(p.q + k))
            self.links.send(self.view(base, 0, p.c), self.zs.at[base + k], self.zr.at[base + k], device)

    def to_other_group(self):
        p = self.place
        self.links.send(self.view(0, 0, p.c), self.zs.at[4], self.zr.at[4], p.at(zl=(1 - p.g) * 4 + p.q))

    def to_x_and_core(self, index):
        p = self.place
        for step in (1, 3, 2):
            self.links.send(
                self.view(index, 0, p.c), self.xs.at[index, step], self.xr.at[index, step], p.at(x=mod4(p.x + step))
            )
        self.links.send(self.view(index, 0, p.c), self.cs.at[index], self.cr.at[index], p.at(c=1 - p.c))

    def z_arrive(self, index):
        p = self.place
        self.links.arrive(self.view(index, 0, p.c), self.zs.at[index], self.zr.at[index], p.at(c=1 - p.c))

    def x_arrive(self, step, half):
        p = self.place
        for index in range(4 * half, 4 * half + 4):
            self.links.arrive(
                self.view(index, step, p.c), self.xs.at[index, step], self.xr.at[index, step], p.at(c=1 - p.c)
            )

    def group_view(self, step, half, core):
        group = self.place.g if half == 0 else 1 - self.place.g
        return self.batch(self.x_source(step) * 8 + group * 4, core)

    def x_to_core(self, step, half):
        p = self.place
        slot = 8 + (step - 1) * 2 + half
        self.links.send(self.group_view(step, half, p.c), self.cs.at[slot], self.cr.at[slot], p.at(c=1 - p.c))

    def core_arrive(self, step):
        p = self.place
        if step == 0:
            for index in range(8):
                self.links.arrive(self.view(index, 0, 1 - p.c), self.cs.at[index], self.cr.at[index], p.at(c=1 - p.c))
        else:
            for half in (0, 1):
                slot = 8 + (step - 1) * 2 + half
                self.links.arrive(
                    self.group_view(step, half, 1 - p.c), self.cs.at[slot], self.cr.at[slot], p.at(c=1 - p.c)
                )


class Heads:
    def __init__(self, links, place, piece, ss, rs):
        self.links, self.place, self.piece, self.ss, self.rs = links, place, piece, ss, rs

    def to_y(self, far):
        p = self.place
        slot = p.y * 2 + (1 - p.zh if far else p.zh)
        for step in (1, 3, 2):
            index = far * 4 + step
            self.links.send(self.piece(slot), self.ss.at[index], self.rs.at[index], p.at(y=mod4(p.y + step)))

    def to_far(self):
        p = self.place
        self.links.send(self.piece(p.y * 2 + p.zh), self.ss.at[0], self.rs.at[0], p.at(zh=1 - p.zh))

    def far_arrive(self):
        p = self.place
        self.links.arrive(self.piece(p.y * 2 + 1 - p.zh), self.ss.at[0], self.rs.at[0], p.at(zh=1 - p.zh))

    def y_arrive(self, far):
        p = self.place
        for step in (1, 3, 2):
            index = far * 4 + step
            slot = mod4(p.y - step) * 2 + (1 - p.zh if far else p.zh)
            self.links.arrive(self.piece(slot), self.ss.at[index], self.rs.at[index], p.at(c=1 - p.c))


class Place:
    def __init__(self):
        dp, mp = lax.axis_index("dp"), lax.axis_index("mp")
        self.dp, self.mp = dp, mp
        self.x, self.zl, self.c = lax.div(dp, 16), lax.rem(lax.div(dp, 2), 8), lax.rem(dp, 2)
        self.g, self.q = lax.div(self.zl, 4), lax.rem(self.zl, 4)
        self.y, self.zh = lax.div(mp, 2), lax.rem(mp, 2)

    def at(self, x=None, zl=None, c=None, y=None, zh=None):
        x = self.x if x is None else x
        zl = self.zl if zl is None else zl
        c = self.c if c is None else c
        y = self.y if y is None else y
        zh = self.zh if zh is None else zh
        return (x * 16 + zl * 2 + c, y * 2 + zh)

    def peers(self):
        found = [self.at(c=1 - self.c)]
        found += [self.at(x=mod4(self.x + k)) for k in (1, 2, 3)]
        found += [self.at(y=mod4(self.y + k)) for k in (1, 2, 3)]
        found += [self.at(zl=self.g * 4 + mod4(self.q + k)) for k in (1, 2, 3)]
        found += [self.at(zl=(1 - self.g) * 4 + self.q), self.at(zh=1 - self.zh)]
        return found


def kernel(
    states_hbm, wqkv_hbm, wout_hbm, ck_hbm, cv_hbm, parents_ref, accept_ref, lengths_ref, perm_ref, freq_ref,
    out_ref, nk_ref, nv_ref,
    wbuf, obuf_w, sbuf, hbuf, abuf, kc, vc, acc, reach_ref, cos_ref, sin_ref, qb, kb, vb,
    loc, zs0, zr0, xs0, xr0, cs0, cr0, zs1, zr1, xs1, xr1, cs1, cr1, ss, rs, as0, ar0, as1, ar1,
):
    p = Place()
    links = Links()
    slot_own = p.x * 8 + p.zl
    local = [
        pltpu.make_async_copy(wqkv_hbm, wbuf.at[:, slot_own, p.c], loc.at[0]),
        pltpu.make_async_copy(states_hbm, sbuf.at[p.mp], loc.at[1]),
        pltpu.make_async_copy(wout_hbm, obuf_w.at[slot_own, p.c], loc.at[2]),
        pltpu.make_async_copy(ck_hbm, kc, loc.at[3]),
        pltpu.make_async_copy(cv_hbm, vc, loc.at[4]),
    ]
    for copy in local:
        copy.start()
    barrier = pltpu.get_barrier_semaphore()
    peers = p.peers()
    for device in peers:
        pl.semaphore_signal(barrier, inc=1, device_id=device, device_id_type=MESH)

    qkv = Gather(
        links, p, lambda slot, core: wbuf.at[:, slot, core],
        lambda slot, core: wbuf.at[:, pl.ds(slot, 4), core], zs0, zr0, xs0, xr0, cs0, cr0,
    )
    proj = Gather(
        links, p, lambda slot, core: obuf_w.at[slot, core],
        lambda slot, core: obuf_w.at[pl.ds(slot, 4), core], zs1, zr1, xs1, xr1, cs1, cr1,
    )
    rows = Heads(links, p, lambda slot: sbuf.at[slot], ss, rs)
    mixed = [
        Heads(links, p, lambda slot: abuf.at[slot, 0], as0, ar0),
        Heads(links, p, lambda slot: abuf.at[slot, 1], as1, ar1),
    ]

    local[0].wait()
    local[1].wait()
    local[2].wait()
    pl.semaphore_wait(barrier, len(peers))

    rows.to_far()
    qkv.to_other_group()
    qkv.to_group(0)
    qkv.to_x_and_core(0)
    rows.to_y(0)

    tree = 64
    row_id = lax.broadcasted_iota(jnp.int32, (tree, tree), 0)
    col_id = lax.broadcasted_iota(jnp.int32, (tree, tree), 1)
    col_f = col_id.astype(F32)
    own_len = []
    for r in range(2):
        own_len.append(lengths_ref[perm_ref[p.dp * 2 + r]])
        line = parents_ref[r : r + 1, :].astype(F32)
        column = jnp.sum(jnp.where(row_id == col_id, line, 0.0), axis=1, keepdims=True)
        linked = jnp.where((column == col_f) & (row_id > 0), 1.0, 0.0)
        reach = jnp.where(row_id == col_id, 1.0, 0.0) + linked
        for _ in range(6):
            half = reach.astype(BF16)
            reach = jnp.minimum(jnp.dot(half, half, preferred_element_type=F32), 1.0)
        reach_ref[r] = reach
        depth = jnp.sum(reach, axis=1, keepdims=True) - 1.0
        position = own_len[r].astype(F32) + depth
        angle = position * freq_ref[...]
        lane = lax.broadcasted_iota(jnp.int32, (tree, HEAD_DIM), 1)
        sine = jnp.sin(angle)
        cos_ref[r] = jnp.cos(angle)
        sin_ref[r] = jnp.where(lane < HEAD_DIM // 2, -sine, sine)

    for index in (1, 2, 3):
        qkv.z_arrive(index)
        qkv.to_x_and_core(index)
    qkv.z_arrive(4)
    qkv.to_group(4)
    qkv.to_x_and_core(4)
    rows.far_arrive()
    rows.to_y(1)
    proj.to_other_group()
    proj.to_group(0)
    for index in (5, 6, 7):
        qkv.z_arrive(index)
        qkv.to_x_and_core(index)
    for half in (0, 1):
        for step in (1, 3, 2):
            qkv.x_arrive(step, half)
            qkv.x_to_core(step, half)

    rows.y_arrive(0)
    rows.y_arrive(1)
    flat, width = 128, 256
    total = jnp.zeros((flat, 1), F32)
    for m in range(8):
        total = total + jnp.sum(sbuf[m].reshape(flat, width).astype(F32), axis=1, keepdims=True)
    mean = total / 2048.0
    total = jnp.zeros((flat, 1), F32)
    for m in range(8):
        centred = sbuf[m].reshape(flat, width).astype(F32) - mean
        total = total + jnp.sum(centred * centred, axis=1, keepdims=True)
    inverse = lax.rsqrt(total / 2048.0 + EPSILON)
    for m in range(8):
        centred = sbuf[m].reshape(flat, width).astype(F32) - mean
        hbuf[:, m * width : (m + 1) * width] = (centred * inverse).astype(BF16)

    for step in (0, 1, 3, 2):
        qkv.core_arrive(step)
        xx = mod4(p.x - step)
        part = hbuf[:, pl.ds(pl.multiple_of(xx * 512, 512), 512)]
        for j in range(3):
            block = wbuf[j, pl.ds(xx * 8, 8)].reshape(512, width)
            product = jnp.dot(part, block, preferred_element_type=F32)
            if step == 0:
                acc[j] = product
            else:
                acc[j] = acc[j] + product

    proj.to_x_and_core(0)
    for index in (1, 2, 3):
        proj.z_arrive(index)
        proj.to_x_and_core(index)
    proj.z_arrive(4)
    proj.to_group(4)
    proj.to_x_and_core(4)

    local[3].wait()
    local[4].wait()
    scale = HEAD_DIM ** (-0.5)
    slots = lax.broadcasted_iota(jnp.int32, (tree, 384), 1)
    across = (((1,), (1,)), ((), ()))
    for head in range(2):
        lanes = slice(head * HEAD_DIM, (head + 1) * HEAD_DIM)
        for r in range(2):
            span = slice(r * tree, (r + 1) * tree)
            cosine, sine = cos_ref[r], sin_ref[r]

            def turned(j):
                value = acc[j, span, lanes]
                return (value * cosine + pltpu.roll(value, HEAD_DIM // 2, 1) * sine).astype(BF16)

            queries, keys, values = turned(0), turned(1), acc[2, span, lanes].astype(BF16)
            kb[r, :, lanes] = keys
            vb[r, :, lanes] = values
            cache = lax.dot_general(queries, kc[r, :, lanes], across, preferred_element_type=F32) * scale
            cache = jnp.where(slots < own_len[r], cache, NEG_FILL)
            nodes = lax.dot_general(queries, keys, across, preferred_element_type=F32) * scale
            nodes = jnp.where(reach_ref[r] > 0, nodes, NEG_FILL)
            peak = jnp.maximum(jnp.max(cache, axis=1, keepdims=True), jnp.max(nodes, axis=1, keepdims=True))
            cache = jnp.exp(cache - peak)
            nodes = jnp.exp(nodes - peak)
            denom = jnp.sum(cache, axis=1, keepdims=True) + jnp.sum(nodes, axis=1, keepdims=True)
            cache = (cache / denom).astype(BF16)
            nodes = (nodes / denom).astype(BF16)
            blend = jnp.dot(cache, vc[r, :, lanes], preferred_element_type=F32)
            blend = blend + jnp.dot(nodes, values, preferred_element_type=F32)
            abuf[p.mp, head, span, :] = blend.astype(BF16)
        mixed[head].to_far()
        mixed[head].to_y(0)

    for index in (5, 6, 7):
        proj.z_arrive(index)
        proj.to_x_and_core(index)

    for r in range(2):
        line = accept_ref[r : r + 1, :].astype(F32)
        small_row = lax.broadcasted_iota(jnp.int32, (8, 8), 0)
        small_col = lax.broadcasted_iota(jnp.int32, (8, 8), 1)
        column = jnp.sum(jnp.where(small_row == small_col, line, 0.0), axis=1, keepdims=True)
        picker = jnp.where(column == lax.broadcasted_iota(jnp.int32, (8, tree), 1).astype(F32), 1.0, 0.0).astype(BF16)
        nk_ref[r] = jnp.dot(picker, kb[r], preferred_element_type=F32).astype(BF16)
        nv_ref[r] = jnp.dot(picker, vb[r], preferred_element_type=F32).astype(BF16)

    for half in (0, 1):
        for step in (1, 3, 2):
            proj.x_arrive(step, half)
            proj.x_to_core(step, half)
    for step in (0, 1, 3, 2):
        proj.core_arrive(step)
    for head in range(2):
        mixed[head].far_arrive()
        mixed[head].to_y(1)
    for far in (0, 1):
        for head in range(2):
            mixed[head].y_arrive(far)

    result = sbuf[p.mp].reshape(flat, width).astype(F32)
    product = jnp.zeros((flat, width), F32)
    for m in range(8):
        both = jnp.concatenate([abuf[m, 0], abuf[m, 1]], axis=1)
        block = obuf_w[4 * m : 4 * m + 4].reshape(256, width)
        product = product + jnp.dot(both, block, preferred_element_type=F32)
    out_ref[...] = (result + product).astype(BF16).reshape(2, tree, width)
    links.drain()


def local(states, w_qkv, w_out, cache_keys, cache_values, parents, accept, lengths, perm):
    half = HEAD_DIM // 2
    freqs = ROPE_BASE ** (-(np.arange(half, dtype=np.float32) * np.float32(2.0) / np.float32(HEAD_DIM)))
    freqs = np.concatenate([freqs, freqs]).astype(np.float32)[None, :]
    hbm = pl.BlockSpec(memory_space=pl.ANY)
    vmem = pl.BlockSpec(memory_space=pltpu.VMEM)
    smem = pl.BlockSpec(memory_space=pltpu.SMEM)
    dma = pltpu.SemaphoreType.DMA
    gather_sems = [dma((8,)), dma((8,)), dma((8, 4)), dma((8, 4)), dma((14,)), dma((14,))]
    return pl.pallas_call(
        kernel,
        name="sublayer",
        out_shape=(
            jax.ShapeDtypeStruct((2, 64, 256), BF16),
            jax.ShapeDtypeStruct((2, 8, 256), BF16),
            jax.ShapeDtypeStruct((2, 8, 256), BF16),
        ),
        in_specs=[hbm, hbm, hbm, hbm, hbm, vmem, vmem, smem, smem, vmem],
        out_specs=(vmem, vmem, vmem),
        scratch_shapes=[
            pltpu.VMEM((3, 32, 2, 32, 256), BF16),
            pltpu.VMEM((32, 2, 32, 256), BF16),
            pltpu.VMEM((8, 2, 64, 256), BF16),
            pltpu.VMEM((128, 2048), BF16),
            pltpu.VMEM((8, 2, 128, 128), BF16),
            pltpu.VMEM((2, 384, 256), BF16),
            pltpu.VMEM((2, 384, 256), BF16),
            pltpu.VMEM((3, 128, 256), F32),
            pltpu.VMEM((2, 64, 64), F32),
            pltpu.VMEM((2, 64, 128), F32),
            pltpu.VMEM((2, 64, 128), F32),
            pltpu.VMEM((2, 64, 256), BF16),
            pltpu.VMEM((2, 64, 256), BF16),
            pltpu.VMEM((2, 64, 256), BF16),
            dma((5,)), *gather_sems, *gather_sems,
            dma((8,)), dma((8,)), dma((8,)), dma((8,)), dma((8,)), dma((8,)),
        ],
        compiler_params=pltpu.CompilerParams(collective_id=0, has_side_effects=True),
    )(states, w_qkv, w_out, cache_keys, cache_values, parents, accept, lengths, perm, jnp.asarray(freqs))


def solution(mesh):
    in_specs = (
        P("dp", None, "mp"),
        P(None, "dp", "mp"),
        P("dp", "mp"),
        P("dp", None, "mp"),
        P("dp", None, "mp"),
        P("dp", None),
        P("dp", None),
        P(),
        P(),
    )
    out_specs = (P("dp", None, "mp"), P("dp", None, "mp"), P("dp", None, "mp"))
    return jax.shard_map(local, mesh=mesh, in_specs=in_specs, out_specs=out_specs, check_vma=False)
```

time: 534 us -> 73.8 us (0.14)
  the two profiles are of different devices: /device:TPU:6 before, /device:TPU:1 now
where the time goes in v1:
time: 73.8 us; the launch traced here: 73.6 us
  Pallas kernels  70.1 us (95%)
  local copies, waits for them, and re-layouts  2.78 us (4%)
    pallas_call x1, Pallas kernels, local(): pl.pallas_call(kernel, name='sublayer', out_shape=(jax.ShapeDtypeStruct((...  70.1 us
    unnamed x7, local copies, waits for them, and re-layouts  2.78 us

profile of v1, /device:TPU:1, one launch (start us, length us, event | category | flops | bytes accessed | tf_op | source)
XLA Modules:
  0.0 73.6 jit_solution(7408202388813852530)
XLA Ops:
  0.6 70.1 %sublayer.1 = (bf16[2,64,256]{2,1,0:T(8,128)(2,1)}, bf16[2,8,256]{2,1,0:T(8,128)(2,1)}, bf16[2,8,256]{2,1,0:T(8,128)(2,1)}) custom-call(bf16[2,64,256]{2,1,0:T(8,128)(2,1)} %states_hbm.1, bf16[3,32,256]{2,1,0:T(8,128)(2,1)} %wqkv_hbm.1, bf16[32,256]{1,0:T(8,128)(2,1)} %wout_hbm.1, bf16[2,384,256]{2,1,0:T(8,128)(2,1)} %ck_hbm.1, bf16[2,384,256]{2,1,0:T(8,128)(2,1)} %cv_hbm.1, ...), custom_call_target="tpu_custom_call" | custom-call | tf_op jit(solution)/shard_map/sublayer/pallas_call | solution.py:370
  70.8 0.0 copy-start.1
  70.8 1.5 %copy.16 = bf16[2,64,256]{2,1,0:T(8,128)(2,1)} copy(bf16[2,64,256]{2,1,0:T(8,128)(2,1)} %get-tuple-element.6) | data formatting | bytes 131072
  72.2 0.0 copy-done.1
  72.3 0.0 copy-start
  72.3 0.6 copy.17
  72.9 0.1 copy-done
  73.0 0.6 copy.18
Async XLA Ops:
  70.8 1.5 %copy-start.1 = (bf16[2,8,256]{2,1,0:T(8,128)(2,1)S(1)}, bf16[2,8,256]{2,1,0:T(8,128)(2,1)}, u32[]{:S(2)}) copy-start(bf16[2,8,256]{2,1,0:T(8,128)(2,1)} %get-tuple-element.7) | copy-start | bytes 24580
  72.3 0.7 copy-start

commit v2 on v1

--- a/solution.py
+++ b/solution.py
@@ -154,12 +154,15 @@
         zh = self.zh if zh is None else zh
         return (x * 16 + zl * 2 + c, y * 2 + zh)
 
+    def middle(self):
+        return self.at(zl=(1 - self.g) * 4 + self.q, zh=1 - self.zh)
+
     def peers(self):
         found = [self.at(c=1 - self.c)]
         found += [self.at(x=mod4(self.x + k)) for k in (1, 2, 3)]
         found += [self.at(y=mod4(self.y + k)) for k in (1, 2, 3)]
         found += [self.at(zl=self.g * 4 + mod4(self.q + k)) for k in (1, 2, 3)]
-        found += [self.at(zl=(1 - self.g) * 4 + self.q), self.at(zh=1 - self.zh)]
+        found += [self.at(zl=(1 - self.g) * 4 + self.q), self.middle()]
         return found
 
 
@@ -167,7 +170,7 @@
     states_hbm, wqkv_hbm, wout_hbm, ck_hbm, cv_hbm, parents_ref, accept_ref, lengths_ref, perm_ref, freq_ref,
     out_ref, nk_ref, nv_ref,
     wbuf, obuf_w, sbuf, hbuf, abuf, kc, vc, acc, reach_ref, cos_ref, sin_ref, qb, kb, vb,
-    loc, zs0, zr0, xs0, xr0, cs0, cr0, zs1, zr1, xs1, xr1, cs1, cr1, ss, rs, as0, ar0, as1, ar1,
+    loc, zs0, zr0, xs0, xr0, cs0, cr0, zs1, zr1, xs1, xr1, cs1, cr1, ss, rs, as0, ar0, as1, ar1, far_ok,
 ):
     p = Place()
     links = Links()
@@ -201,14 +204,13 @@
     ]
 
     local[0].wait()
-    local[1].wait()
-    local[2].wait()
     pl.semaphore_wait(barrier, len(peers))
-
-    rows.to_far()
+    pl.semaphore_signal(far_ok, inc=1, device_id=p.middle(), device_id_type=MESH)
+
     qkv.to_other_group()
     qkv.to_group(0)
     qkv.to_x_and_core(0)
+    local[1].wait()
     rows.to_y(0)
 
     tree = 64
@@ -240,17 +242,28 @@
     qkv.z_arrive(4)
     qkv.to_group(4)
     qkv.to_x_and_core(4)
-    rows.far_arrive()
-    rows.to_y(1)
-    proj.to_other_group()
-    proj.to_group(0)
     for index in (5, 6, 7):
         qkv.z_arrive(index)
         qkv.to_x_and_core(index)
-    for half in (0, 1):
-        for step in (1, 3, 2):
-            qkv.x_arrive(step, half)
-            qkv.x_to_core(step, half)
+    pl.semaphore_wait(far_ok, 1)
+    rows.to_far()
+    local[2].wait()
+    proj.to_other_group()
+    proj.to_group(0)
+    for step in (1, 3, 2):
+        qkv.x_arrive(step, 0)
+        qkv.x_to_core(step, 0)
+    rows.far_arrive()
+    rows.to_y(1)
+    for index in (1, 2, 3):
+        proj.z_arrive(index)
+    proj.z_arrive(4)
+    proj.to_group(4)
+    for step in (1, 3, 2):
+        qkv.x_arrive(step, 1)
+        qkv.x_to_core(step, 1)
+    for index in (0, 1, 2, 3, 4):
+        proj.to_x_and_core(index)
 
     rows.y_arrive(0)
     rows.y_arrive(1)
@@ -268,6 +281,10 @@
         centred = sbuf[m].reshape(flat, width).astype(F32) - mean
         hbuf[:, m * width : (m + 1) * width] = (centred * inverse).astype(BF16)
 
+    for index in (5, 6, 7):
+        proj.z_arrive(index)
+        proj.to_x_and_core(index)
+
     for step in (0, 1, 3, 2):
         qkv.core_arrive(step)
         xx = mod4(p.x - step)
@@ -279,14 +296,6 @@
                 acc[j] = product
             else:
                 acc[j] = acc[j] + product
-
-    proj.to_x_and_core(0)
-    for index in (1, 2, 3):
-        proj.z_arrive(index)
-        proj.to_x_and_core(index)
-    proj.z_arrive(4)
-    proj.to_group(4)
-    proj.to_x_and_core(4)
 
     local[3].wait()
     local[4].wait()
@@ -322,10 +331,6 @@
         mixed[head].to_far()
         mixed[head].to_y(0)
 
-    for index in (5, 6, 7):
-        proj.z_arrive(index)
-        proj.to_x_and_core(index)
-
     for r in range(2):
         line = accept_ref[r : r + 1, :].astype(F32)
         small_row = lax.broadcasted_iota(jnp.int32, (8, 8), 0)
@@ -341,20 +346,26 @@
             proj.x_to_core(step, half)
     for step in (0, 1, 3, 2):
         proj.core_arrive(step)
+    product = sbuf[p.mp].reshape(flat, width).astype(F32)
+
+    def projected(m):
+        both = jnp.concatenate([abuf[m, 0], abuf[m, 1]], axis=1)
+        block = obuf_w[pl.ds(4 * m, 4)].reshape(256, width)
+        return jnp.dot(both, block, preferred_element_type=F32)
+
+    for head in range(2):
+        mixed[head].y_arrive(0)
+    for step in (0, 1, 3, 2):
+        product = product + projected(mod4(p.y - step) * 2 + p.zh)
     for head in range(2):
         mixed[head].far_arrive()
         mixed[head].to_y(1)
-    for far in (0, 1):
-        for head in range(2):
-            mixed[head].y_arrive(far)
-
-    result = sbuf[p.mp].reshape(flat, width).astype(F32)
-    product = jnp.zeros((flat, width), F32)
-    for m in range(8):
-        both = jnp.concatenate([abuf[m, 0], abuf[m, 1]], axis=1)
-        block = obuf_w[4 * m : 4 * m + 4].reshape(256, width)
-        product = product + jnp.dot(both, block, preferred_element_type=F32)
-    out_ref[...] = (result + product).astype(BF16).reshape(2, tree, width)
+    product = product + projected(p.y * 2 + 1 - p.zh)
+    for head in range(2):
+        mixed[head].y_arrive(1)
+    for step in (1, 3, 2):
+        product = product + projected(mod4(p.y - step) * 2 + 1 - p.zh)
+    out_ref[...] = product.astype(BF16).reshape(2, tree, width)
     links.drain()
 
 
@@ -393,7 +404,7 @@
             pltpu.VMEM((2, 64, 256), BF16),
             pltpu.VMEM((2, 64, 256), BF16),
             dma((5,)), *gather_sems, *gather_sems,
-            dma((8,)), dma((8,)), dma((8,)), dma((8,)), dma((8,)), dma((8,)),
+            dma((8,)), dma((8,)), dma((8,)), dma((8,)), dma((8,)), dma((8,)), pltpu.SemaphoreType.REGULAR,
         ],
         compiler_params=pltpu.CompilerParams(collective_id=0, has_side_effects=True),
     )(states, w_qkv, w_out, cache_keys, cache_values, parents, accept, lengths, perm, jnp.asarray(freqs))

time: 73.8 us -> 66.5 us (0.901)
  the two profiles are of different devices: /device:TPU:1 before, /device:TPU:6 now
where the time goes in v2:
time: 66.5 us; the launch traced here: 66.3 us
  Pallas kernels  62.9 us (95%)
  local copies, waits for them, and re-layouts  2.78 us (4%)
    pallas_call x1, Pallas kernels, local(): pl.pallas_call(kernel, name='sublayer', out_shape=(jax.ShapeDtypeStruct((...  62.9 us
    unnamed x7, local copies, waits for them, and re-layouts  2.78 us

profile of v2, /device:TPU:6, one launch (start us, length us, event | category | flops | bytes accessed | tf_op | source)
XLA Modules:
  0.0 66.3 jit_solution(17889761770001365799)
XLA Ops:
  0.6 62.9 %sublayer.1 = (bf16[2,64,256]{2,1,0:T(8,128)(2,1)}, bf16[2,8,256]{2,1,0:T(8,128)(2,1)}, bf16[2,8,256]{2,1,0:T(8,128)(2,1)}) custom-call(bf16[2,64,256]{2,1,0:T(8,128)(2,1)} %states_hbm.1, bf16[3,32,256]{2,1,0:T(8,128)(2,1)} %wqkv_hbm.1, bf16[32,256]{1,0:T(8,128)(2,1)} %wout_hbm.1, bf16[2,384,256]{2,1,0:T(8,128)(2,1)} %ck_hbm.1, bf16[2,384,256]{2,1,0:T(8,128)(2,1)} %cv_hbm.1, ...), custom_call_target="tpu_custom_call" | custom-call | tf_op jit(solution)/shard_map/sublayer/pallas_call | solution.py:381
  63.5 0.0 copy-start.1
  63.5 1.5 %copy.16 = bf16[2,64,256]{2,1,0:T(8,128)(2,1)} copy(bf16[2,64,256]{2,1,0:T(8,128)(2,1)} %get-tuple-element.6) | data formatting | bytes 131072
  65.0 0.0 copy-done.1
  65.0 0.0 copy-start
  65.0 0.6 copy.17
  65.6 0.1 copy-done
  65.7 0.6 copy.18
Async XLA Ops:
  63.5 1.5 %copy-start.1 = (bf16[2,8,256]{2,1,0:T(8,128)(2,1)S(1)}, bf16[2,8,256]{2,1,0:T(8,128)(2,1)}, u32[]{:S(2)}) copy-start(bf16[2,8,256]{2,1,0:T(8,128)(2,1)} %get-tuple-element.7) | copy-start | bytes 24580
  65.0 0.7 %copy-start = (bf16[2,8,256]{2,1,0:T(8,128)(2,1)S(1)}, bf16[2,8,256]{2,1,0:T(8,128)(2,1)}, u32[]{:S(2)}) copy-start(bf16[2,8,256]{2,1,0:T(8,128)(2,1)} %get-tuple-element.8) | copy-start | bytes 24580

commit v3 on v2

--- a/solution.py
+++ b/solution.py
@@ -369,6 +369,12 @@
     links.drain()
 
 
+def hand_out(out_in, nk_in, nv_in, out_ref, nk_ref, nv_ref):
+    out_ref[...] = out_in[...]
+    nk_ref[...] = nk_in[...]
+    nv_ref[...] = nv_in[...]
+
+
 def local(states, w_qkv, w_out, cache_keys, cache_values, parents, accept, lengths, perm):
     half = HEAD_DIM // 2
     freqs = ROPE_BASE ** (-(np.arange(half, dtype=np.float32) * np.float32(2.0) / np.float32(HEAD_DIM)))
@@ -378,14 +384,15 @@
     smem = pl.BlockSpec(memory_space=pltpu.SMEM)
     dma = pltpu.SemaphoreType.DMA
     gather_sems = [dma((8,)), dma((8,)), dma((8, 4)), dma((8, 4)), dma((14,)), dma((14,))]
-    return pl.pallas_call(
+    shapes = (
+        jax.ShapeDtypeStruct((2, 64, 256), BF16),
+        jax.ShapeDtypeStruct((2, 8, 256), BF16),
+        jax.ShapeDtypeStruct((2, 8, 256), BF16),
+    )
+    results = pl.pallas_call(
         kernel,
         name="sublayer",
-        out_shape=(
-            jax.ShapeDtypeStruct((2, 64, 256), BF16),
-            jax.ShapeDtypeStruct((2, 8, 256), BF16),
-            jax.ShapeDtypeStruct((2, 8, 256), BF16),
-        ),
+        out_shape=shapes,
         in_specs=[hbm, hbm, hbm, hbm, hbm, vmem, vmem, smem, smem, vmem],
         out_specs=(vmem, vmem, vmem),
         scratch_shapes=[
@@ -408,6 +415,7 @@
         ],
         compiler_params=pltpu.CompilerParams(collective_id=0, has_side_effects=True),
     )(states, w_qkv, w_out, cache_keys, cache_values, parents, accept, lengths, perm, jnp.asarray(freqs))
+    return pl.pallas_call(hand_out, name="hand_out", out_shape=shapes, in_specs=[vmem] * 3, out_specs=(vmem,) * 3)(*results)
 
 
 def solution(mesh):

time: 66.5 us -> 65.2 us (0.980)
  local copies, waits for them, and re-layouts: 2.78 us -> 0 us
  Pallas kernels: 62.9 us -> 64.4 us
    unnamed x7 -> x0, local copies, waits for them, and re-layouts: 2.78 us -> none
    pallas_call x1 -> x2, Pallas kernels: 62.9 us -> 64.4 us  [the longest x1 62.9 us: local(): pl.pallas_call(kernel, name='sublayer', out_shape=shapes, in_specs=[hbm,...]
where the time goes in v3:
time: 65.2 us; the launch traced here: 65 us
  Pallas kernels  64.4 us (99%)
    pallas_call x1, Pallas kernels, local(): pl.pallas_call(kernel, name='sublayer', out_shape=shapes, in_specs=[hbm,...  62.9 us
    pallas_call x1, Pallas kernels, local(): pl.pallas_call(hand_out, name='hand_out', out_shape=shapes, in_specs=[vme...  1.5 us

profile of v3, /device:TPU:6, one launch (start us, length us, event | category | flops | bytes accessed | tf_op | source)
XLA Modules:
  0.0 65.0 jit_solution(4461088227667304420)
XLA Ops:
  0.6 62.9 %sublayer.1 = (bf16[2,64,256]{2,1,0:T(8,128)(2,1)}, bf16[2,8,256]{2,1,0:T(8,128)(2,1)}, bf16[2,8,256]{2,1,0:T(8,128)(2,1)}) custom-call(bf16[2,64,256]{2,1,0:T(8,128)(2,1)} %states_hbm.1, bf16[3,32,256]{2,1,0:T(8,128)(2,1)} %wqkv_hbm.1, bf16[32,256]{1,0:T(8,128)(2,1)} %wout_hbm.1, bf16[2,384,256]{2,1,0:T(8,128)(2,1)} %ck_hbm.1, bf16[2,384,256]{2,1,0:T(8,128)(2,1)} %cv_hbm.1, ...), custom_call_target="tpu_custom_call" | custom-call | tf_op jit(solution)/shard_map/sublayer/pallas_call | solution.py:392
  63.5 1.5 %hand_out.1 = (bf16[2,64,256]{2,1,0:T(8,128)(2,1)}, bf16[2,8,256]{2,1,0:T(8,128)(2,1)}, bf16[2,8,256]{2,1,0:T(8,128)(2,1)}) custom-call(bf16[2,64,256]{2,1,0:T(8,128)(2,1)} %get-tuple-element.6.out_in, bf16[2,8,256]{2,1,0:T(8,128)(2,1)} %get-tuple-element.7.nk_in, bf16[2,8,256]{2,1,0:T(8,128)(2,1)} %get-tuple-element.8.nv_in), custom_call_target="tpu_custom_call" | custom-call | tf_op jit(solution)/shard_map/hand_out/pallas_call | solution.py:418

commit v4 on v3

--- a/solution.py
+++ b/solution.py
@@ -25,9 +25,9 @@
     def __init__(self):
         self.started = []
 
-    def send(self, view, send_sem, recv_sem, device):
+    def send(self, view, send_sem, recv_sem, device, source=None):
         copy = pltpu.make_async_remote_copy(
-            src_ref=view, dst_ref=view, send_sem=send_sem, recv_sem=recv_sem,
+            src_ref=view if source is None else source, dst_ref=view, send_sem=send_sem, recv_sem=recv_sem,
             device_id=device, device_id_type=MESH,
         )
         copy.start()
@@ -45,7 +45,8 @@
 
 
 class Gather:
-    def __init__(self, links, place, shard, batch, zs, zr, xs, xr, cs, cr):
+    def __init__(self, links, place, own, shard, batch, zs, zr, xs, xr, cs, cr):
+        self.own = own
         self.links, self.place, self.shard, self.batch = links, place, shard, batch
         self.zs, self.zr, self.xs, self.xr, self.cs, self.cr = zs, zr, xs, xr, cs, cr
 
@@ -60,23 +61,27 @@
     def view(self, index, step, core):
         return self.shard(self.x_source(step) * 8 + self.z_source(index), core)
 
+    def source(self, index):
+        return self.own if index == 0 else None
+
     def to_group(self, base):
         p = self.place
         for k in (1, 2, 3):
             device = p.at(zl=p.g * 4 + mod4(p.q + k))
-            self.links.send(self.view(base, 0, p.c), self.zs.at[base + k], self.zr.at[base + k], device)
+            self.links.send(self.view(base, 0, p.c), self.zs.at[base + k], self.zr.at[base + k], device, self.source(base))
 
     def to_other_group(self):
         p = self.place
-        self.links.send(self.view(0, 0, p.c), self.zs.at[4], self.zr.at[4], p.at(zl=(1 - p.g) * 4 + p.q))
+        self.links.send(self.view(0, 0, p.c), self.zs.at[4], self.zr.at[4], p.at(zl=(1 - p.g) * 4 + p.q), self.own)
 
     def to_x_and_core(self, index):
         p = self.place
-        for step in (1, 3, 2):
+        for step in (2, 1, 3):
             self.links.send(
-                self.view(index, 0, p.c), self.xs.at[index, step], self.xr.at[index, step], p.at(x=mod4(p.x + step))
+                self.view(index, 0, p.c), self.xs.at[index, step], self.xr.at[index, step], p.at(x=mod4(p.x + step)),
+                self.source(index),
             )
-        self.links.send(self.view(index, 0, p.c), self.cs.at[index], self.cr.at[index], p.at(c=1 - p.c))
+        self.links.send(self.view(index, 0, p.c), self.cs.at[index], self.cr.at[index], p.at(c=1 - p.c), self.source(index))
 
     def z_arrive(self, index):
         p = self.place
@@ -118,7 +123,7 @@
     def to_y(self, far):
         p = self.place
         slot = p.y * 2 + (1 - p.zh if far else p.zh)
-        for step in (1, 3, 2):
+        for step in (2, 1, 3):
             index = far * 4 + step
             self.links.send(self.piece(slot), self.ss.at[index], self.rs.at[index], p.at(y=mod4(p.y + step)))
 
@@ -190,11 +195,11 @@
         pl.semaphore_signal(barrier, inc=1, device_id=device, device_id_type=MESH)
 
     qkv = Gather(
-        links, p, lambda slot, core: wbuf.at[:, slot, core],
+        links, p, wqkv_hbm, lambda slot, core: wbuf.at[:, slot, core],
         lambda slot, core: wbuf.at[:, pl.ds(slot, 4), core], zs0, zr0, xs0, xr0, cs0, cr0,
     )
     proj = Gather(
-        links, p, lambda slot, core: obuf_w.at[slot, core],
+        links, p, wout_hbm, lambda slot, core: obuf_w.at[slot, core],
         lambda slot, core: obuf_w.at[pl.ds(slot, 4), core], zs1, zr1, xs1, xr1, cs1, cr1,
     )
     rows = Heads(links, p, lambda slot: sbuf.at[slot], ss, rs)
@@ -203,7 +208,6 @@
         Heads(links, p, lambda slot: abuf.at[slot, 1], as1, ar1),
     ]
 
-    local[0].wait()
     pl.semaphore_wait(barrier, len(peers))
     pl.semaphore_signal(far_ok, inc=1, device_id=p.middle(), device_id_type=MESH)
 
@@ -247,7 +251,6 @@
         qkv.to_x_and_core(index)
     pl.semaphore_wait(far_ok, 1)
     rows.to_far()
-    local[2].wait()
     proj.to_other_group()
     proj.to_group(0)
     for step in (1, 3, 2):
@@ -285,6 +288,8 @@
         proj.z_arrive(index)
         proj.to_x_and_core(index)
 
+    local[0].wait()
+    local[2].wait()
     for step in (0, 1, 3, 2):
         qkv.core_arrive(step)
         xx = mod4(p.x - step)

time: 65.2 us -> 65 us (level)
  the two profiles are of different devices: /device:TPU:6 before, /device:TPU:4 now
where the time goes in v4:
time: 65 us; the launch traced here: 64.8 us
  Pallas kernels  64.2 us (99%)
    pallas_call x1, Pallas kernels, local(): pl.pallas_call(kernel, name='sublayer', out_shape=shapes, in_specs=[hbm,...  62.7 us
    pallas_call x1, Pallas kernels, local(): pl.pallas_call(hand_out, name='hand_out', out_shape=shapes, in_specs=[vme...  1.5 us

profile of v4, /device:TPU:4, one launch (start us, length us, event | category | flops | bytes accessed | tf_op | source)
XLA Modules:
  0.0 64.8 jit_solution(11918630959814053904)
XLA Ops:
  0.6 62.7 %sublayer.1 = (bf16[2,64,256]{2,1,0:T(8,128)(2,1)}, bf16[2,8,256]{2,1,0:T(8,128)(2,1)}, bf16[2,8,256]{2,1,0:T(8,128)(2,1)}) custom-call(bf16[2,64,256]{2,1,0:T(8,128)(2,1)} %states_hbm.1, bf16[3,32,256]{2,1,0:T(8,128)(2,1)} %wqkv_hbm.1, bf16[32,256]{1,0:T(8,128)(2,1)} %wout_hbm.1, bf16[2,384,256]{2,1,0:T(8,128)(2,1)} %ck_hbm.1, bf16[2,384,256]{2,1,0:T(8,128)(2,1)} %cv_hbm.1, ...), custom_call_target="tpu_custom_call" | custom-call | tf_op jit(solution)/shard_map/sublayer/pallas_call | solution.py:397
  63.3 1.5 %hand_out.1 = (bf16[2,64,256]{2,1,0:T(8,128)(2,1)}, bf16[2,8,256]{2,1,0:T(8,128)(2,1)}, bf16[2,8,256]{2,1,0:T(8,128)(2,1)}) custom-call(bf16[2,64,256]{2,1,0:T(8,128)(2,1)} %get-tuple-element.6.out_in, bf16[2,8,256]{2,1,0:T(8,128)(2,1)} %get-tuple-element.7.nk_in, bf16[2,8,256]{2,1,0:T(8,128)(2,1)} %get-tuple-element.8.nv_in), custom_call_target="tpu_custom_call" | custom-call | tf_op jit(solution)/shard_map/hand_out/pallas_call | solution.py:423
